TPU v7x, 128 devices: a whole 4x4x4 slice. The times are simulated.
128 devices in a mesh: row: 8 (over x, z_lo), col: 16 (over y, z_hi, core).
Axes of the slice: x: 4, y: 4, z: 4 (z_hi: 2, z_lo: 2; z = z_hi * 2 + z_lo), core: 2. Of those that a mesh axis runs over, the one named last changes fastest.
Arguments:
- sib_inverse: bfloat16 [24576, 12288], P('row', 'col'), may hold values from -0.0546875 to 0.0546875
- sib_panel: bfloat16 [24576, 512], P(('row', 'col')), may hold values from -0.15625 to 0.15625
- sib_cot: bfloat16 [24576, 512], P(('row', 'col')), may hold values from -6 to 6
- par_inverse: bfloat16 [16384, 16384], P('row', 'col'), may hold values from -0.046875 to 0.046875
- par_panel: bfloat16 [16384, 512], P(('row', 'col')), may hold values from -0.15625 to 0.15625
- par_cot: bfloat16 [16384, 512], P(('row', 'col')), may hold values from -6 to 6
- block_map: int32 [2, 96], replicated, may hold values from 0 to 127, as said below
- row_mask: int32 [24576], replicated, may hold values 0 or 1
Outputs:
- sib_grad: float32 [12288, 1024], P('col', 'row')
- par_grad: float32 [16384, 512], P('col', 'row')
- border_grad: float32 [16384, 16384], P('row', 'col')
Inputs may be any that keep to these rules, and one draw needn't show every extreme that they name: In each row of block_map the values are distinct. Among the 24 blocks k * 24 to (k + 1) * 24 - 1 of one sibling, at most 4 have values in one range q * 16 to (q + 1) * 16 - 1, and for every k some range holds exactly 4 of them.
All inputs are finite; a program needn't handle non-finite values.
Results may differ from a plain program's by a relative error of at most 0.0003.
Values may be sent and summed in bfloat16 or wider, within the bound.
A program may use at most 128 MiB of HBM per device.

v0:
```python
import jax
import jax.numpy as jnp
from jax import lax
from jax.sharding import PartitionSpec as P

BLK = 128


def in_one_piece(arrays, axis, dim, along):
    ends, at = ([], 0)
    for a in arrays[:-1]:
        at += a.shape[along]
        ends.append(at)
    both = jnp.concatenate(arrays, axis=along)
    return tuple(jnp.split(lax.all_gather(both, axis, axis=dim, tiled=True), ends, axis=along))


def from_partner(block, axis, stride):
    count = lax.axis_size(axis)
    route = []
    for low in range(count):
        high = low | 1 << stride
        if high != low and high < count:
            route += [(low, high), (high, low)]
    return lax.ppermute(block, axis, route)


def cut_along(shard, dim, devices):
    dims = shard.shape
    tiles = shard.reshape(*dims[:dim], devices, dims[dim] // devices, *dims[dim + 1 :])
    return jnp.moveaxis(tiles, dim, 0)


def sent_and_summed(shard, axis, dim):
    tiles = cut_along(shard, dim, lax.axis_size(axis))
    arrived = lax.all_to_all(tiles, axis, split_axis=0, concat_axis=0, tiled=True)
    return arrived.sum(axis=0)


def sent_together(arrays, axis, split_dim, concat_dim, along):
    widths = [a.shape[along] for a in arrays]
    both = jnp.concatenate(arrays, axis=along)
    result = lax.all_to_all(both, axis, split_axis=split_dim, concat_axis=concat_dim, tiled=True)
    return tuple(jnp.split(result, [sum(widths[:k]) for k in range(1, len(widths))], axis=along))


def padded_to(lines, devices):
    spare = -lines.shape[0] % devices
    if not spare:
        return lines
    return jnp.concatenate([lines, jnp.zeros((spare, *lines.shape[1:]), lines.dtype)])


def broadcast_by_parts(shard, axis, root):
    lines = jnp.where(lax.axis_index(axis) == root, shard, jnp.zeros_like(shard)).reshape(
        -1, *shard.shape[1:][-1:]
    )
    padded = padded_to(lines, lax.axis_size(axis))
    own = lax.psum_scatter(padded, axis, scatter_dimension=0, tiled=True)
    return lax.all_gather(own, axis, axis=0, tiled=True)[: len(lines)].reshape(shard.shape)


def arrival_rank(destinations):
    count = destinations.shape[-1]
    row_iota = lax.broadcasted_iota(jnp.int32, (count, count), 0)
    col_iota = lax.broadcasted_iota(jnp.int32, (count, count), 1)
    equal_dest = destinations[..., :, None] == destinations[..., None, :]
    return jnp.sum((equal_dest & (col_iota < row_iota)).astype(jnp.int32), axis=-1)


def on_device(
    sib_inverse, sib_panel, sib_cot, par_inverse, par_panel, par_cot, block_map, row_mask
):
    row_count = lax.axis_size("row")
    col_count = lax.axis_size("col")
    half_rows = row_count // 2
    here_row = lax.axis_index("row")
    here_col = lax.axis_index("col")
    sibling = here_row // half_rows
    row_in_half = here_row % half_rows
    tile_rows, tile_cols = sib_inverse.shape
    border_child = tile_cols * col_count
    pivots = sib_cot.shape[1]
    ptile_rows, ptile_cols = par_inverse.shape
    child_blocks = tile_rows // BLK
    parent_blocks = ptile_rows // BLK
    base_load = child_blocks // row_count
    capacity = base_load + base_load // 2
    slot_count = row_count * capacity
    cot_rows, panel_rows, pcot_rows, ppanel_rows = (
        *in_one_piece((sib_cot, sib_panel), "col", 0, 1),
        *in_one_piece((par_cot, par_panel), "col", 0, 1),
    )
    live_rows = lax.dynamic_slice_in_dim(row_mask, here_row * tile_rows, tile_rows)
    live = live_rows.astype(jnp.bfloat16)[:, None]
    cot_masked = cot_rows * live
    panel_masked = panel_rows * live
    live_cols = lax.dynamic_slice_in_dim(
        row_mask, sibling * border_child + here_col * tile_cols, tile_cols
    ).astype(jnp.float32)[:, None]
    contract = (((0,), (0,)), ((), ()))
    child_part = (
        -lax.dot_general(sib_inverse, cot_masked, contract, preferred_element_type=jnp.float32)
        * live_cols
    )
    parent_part = -lax.dot_general(
        par_inverse, pcot_rows, contract, preferred_element_type=jnp.float32
    )
    current = child_part
    bit_count = half_rows.bit_length() - 1
    for level in reversed(range(bit_count)):
        half_cols = current.shape[1] // 2
        high_side = row_in_half >> level & 1
        lower_cols = current[:, :half_cols]
        upper_cols = current[:, half_cols:]
        outgoing = jnp.where(high_side == 1, lower_cols, upper_cols)
        retained = jnp.where(high_side == 1, upper_cols, lower_cols)
        current = retained + from_partner(outgoing, "row", level)
    par_grad = sent_and_summed(parent_part, "row", 1)
    all_ids = block_map.reshape(row_count, child_blocks)
    all_dest = all_ids // parent_blocks
    all_rank = arrival_rank(all_dest)
    my_dest = lax.dynamic_index_in_dim(all_dest, here_row, 0, keepdims=False)
    my_rank = lax.dynamic_index_in_dim(all_rank, here_row, 0, keepdims=False)
    slot_of = my_dest * capacity + my_rank
    slot_iota = jnp.arange(slot_count, dtype=jnp.int32)
    block_iota = jnp.arange(child_blocks, dtype=jnp.int32)
    matches = slot_of[None, :] == slot_iota[:, None]
    source = jnp.sum(jnp.where(matches, block_iota[None, :], 0), axis=1)
    filled = jnp.any(matches, axis=1)

    def pack_slots(rows):
        blocks = rows.reshape(child_blocks, BLK, pivots)
        picked = jnp.take(blocks, source, axis=0)
        return jnp.where(filled[:, None, None], picked, jnp.zeros_like(picked))

    send_cot = pack_slots(cot_masked)
    send_panel = pack_slots(panel_masked)
    piece_rows = BLK // col_count
    first_row = here_col * piece_rows
    part_cot = lax.dynamic_slice_in_dim(send_cot, first_row, piece_rows, 1)
    part_panel = lax.dynamic_slice_in_dim(send_panel, first_row, piece_rows, 1)
    recv_cot, recv_panel = sent_together((part_cot, part_panel), "row", 0, 0, 1)
    got_cot, got_panel = in_one_piece((recv_cot, recv_panel), "col", 1, 0)
    source_row = jnp.arange(row_count, dtype=jnp.int32)
    target_keys = (source_row // half_rows)[:, None] * parent_blocks + all_ids % parent_blocks
    flat_slot = source_row[:, None] * capacity + all_rank
    to_here = all_dest == here_row
    targets = jnp.arange(2 * parent_blocks, dtype=jnp.int32)
    matched = to_here[None] & (target_keys[None] == targets[:, None, None])
    chosen = jnp.sum(jnp.where(matched, flat_slot[None], 0), axis=(1, 2))
    present = jnp.any(matched, axis=(1, 2))

    def place_blocks(received):
        picked = jnp.take(received, chosen, axis=0)
        placed = jnp.where(present[:, None, None], picked, jnp.zeros_like(picked))
        return placed.reshape(2, parent_blocks * BLK, pivots)

    lifted_cot = place_blocks(got_cot)
    lifted_panel = place_blocks(got_panel)
    row_side = jnp.concatenate([pcot_rows, lifted_cot[0], lifted_cot[1]], axis=1)
    panel_rows_all = jnp.concatenate([ppanel_rows, lifted_panel[0], lifted_panel[1]], axis=1)
    root_row = here_col * ptile_cols // ptile_rows
    offset = jnp.clip(here_col * ptile_cols - here_row * ptile_rows, 0, ptile_rows - ptile_cols)
    outgoing_cols = lax.dynamic_slice_in_dim(panel_rows_all, offset, ptile_cols, 0)
    col_side = broadcast_by_parts(outgoing_cols, "row", root_row)
    border_grad = -lax.dot_general(
        row_side, col_side, (((1,), (1,)), ((), ())), preferred_element_type=jnp.float32
    )
    return (current, par_grad, border_grad)


def solution(mesh):
    placed = (
        P("row", "col"),
        P(("row", "col"), None),
        P(("row", "col"), None),
        P("row", "col"),
        P(("row", "col"), None),
        P(("row", "col"), None),
        P(),
        P(),
    )
    return jax.shard_map(
        on_device,
        mesh=mesh,
        in_specs=placed,
        out_specs=(P("col", "row"), P("col", "row"), P("row", "col")),
        check_vma=False,
    )
```

profile of v0, /device:TPU:1, one launch (start us, length us, event | category | flops | bytes accessed | tf_op | source)
XLA Modules:
  0.0 438.6 jit_solution(5211740346613376897)
XLA Ops:
  7.2 1.8 pad_maximum_fusion.2
  9.1 1.7 pad_maximum_fusion.3
  13.2 65.7 %all-gather.5.cloned.1.call-done = bf16[3072,1024]{1,0:T(8,128)(2,1)} async-done(((bf16[192,1024]{1,0:T(8,128)(2,1)}), bf16[3072,1024]{1,0:T(8,128)(2,1)}) %all-gather.5.cloned.1.call-update) | async-done | bytes 6291472 | tf_op jit(solution)/shard_map/all_gather | solution.py:15
  78.9 4.7 %slice_multiply_fusion = (bf16[3072,512]{1,0:T(8,128)(2,1)}, bf16[3072,512]{1,0:T(8,128)(2,1)S(1)}) fusion(bf16[3072,1024]{1,0:T(8,128)(2,1)} %all-gather.5.cloned.1.call-done, bf16[3072]{0:T(1024)(128)(2,1)S(1)} %dynamic-slice_convert_fusion), kind=kLoop, calls=%fused_computation.19 | loop fusion | flops 3145728 | bytes 12589056 | tf_op jit(solution)/shard_map/mul | solution.py:97
  83.7 4.7 %gather_fusion.1 = bf16[32,128,512]{2,1,0:T(8,128)(2,1)} fusion(bf16[24,128,512]{2,1,0:T(8,128)(2,1)} %bitcast.20, s32[1024]{0:T(1024)S(1)} %pad_clamp_fusion.1), kind=kCustom, calls=%fused_computation.2.clone | custom fusion | bytes 8388736 | tf_op jit(solution)/shard_map/jit(_take)/gather | solution.py:134
  88.3 2.8 gather_fusion
  91.2 1.3 fusion.13
  92.5 12.6 %all_to_all.10 = bf16[32,16,512]{2,1,0:T(8,128)(2,1)S(1)} all-to-all(bf16[32,16,512]{2,1,0:T(8,128)(2,1)S(1)} %pad_maximum_fusion), channel_id=1, replica_groups=mesh['row'=8,'col'=16] {'row'}, dimensions={0} | all-to-all | bytes 1048576 | tf_op jit(solution)/shard_map/all_to_all | solution.py:43
  105.2 0.8 pad_maximum_fusion.1
  106.3 30.0 %all-gather.7.cloned.1.call-done = bf16[2048,1024]{1,0:T(8,128)(2,1)} async-done(((bf16[128,1024]{1,0:T(8,128)(2,1)}), bf16[2048,1024]{1,0:T(8,128)(2,1)}) %all-gather.7.cloned.1.call-update) | async-done | bytes 4194320 | tf_op jit(solution)/shard_map/all_gather | solution.py:15
  136.2 4.4 %fusion.27 = (bf16[2048,512]{1,0:T(8,128)(2,1)}, bf16[2048,512]{1,0:T(8,128)(2,1)}) fusion(bf16[2048,1024]{1,0:T(8,128)(2,1)} %all-gather.7.cloned.1.call-done), kind=kLoop, calls=%fused_computation.77 | loop fusion | bytes 8388608 | tf_op jit(solution)/shard_map/split | solution.py:15
  140.7 77.3 %all-gather.9.cloned.1.call-done = bf16[64,128,512]{2,1,0:T(8,128)(2,1)} async-done(((bf16[64,8,512]{2,1,0:T(8,128)(2,1)}), bf16[64,128,512]{2,1,0:T(8,128)(2,1)}) %all-gather.9.cloned.1.call-update) | async-done | bytes 8388624 | tf_op jit(solution)/shard_map/all_gather | solution.py:15
  218.0 6.0 %fusion.26 = (bf16[32,128,512]{2,1,0:T(8,128)(2,1)}, bf16[32,128,512]{2,1,0:T(8,128)(2,1)}) fusion(bf16[64,128,512]{2,1,0:T(8,128)(2,1)} %all-gather.9.cloned.1.call-done), kind=kLoop, calls=%fused_computation.76 | loop fusion | bytes 16777216 | tf_op jit(solution)/shard_map/split | solution.py:15
  223.9 5.0 %gather_fusion.2 = bf16[32,128,512]{2,1,0:T(8,128)(2,1)} fusion(bf16[32,128,512]{2,1,0:T(8,128)(2,1)} %get-tuple-element.13, s32[1024]{0:T(1024)S(1)} %pad_clamp_fusion), kind=kCustom, calls=%fused_computation.1.clone | custom fusion | bytes 8388736 | tf_op jit(solution)/shard_map/jit(_take)/gather | solution.py:155
  228.9 5.0 %gather_fusion.3 = bf16[32,128,512]{2,1,0:T(8,128)(2,1)} fusion(bf16[32,128,512]{2,1,0:T(8,128)(2,1)} %get-tuple-element.14, s32[1024]{0:T(1024)S(1)} %pad_clamp_fusion), kind=kCustom, calls=%fused_computation.3.clone | custom fusion | bytes 8388736 | tf_op jit(solution)/shard_map/jit(_take)/gather | solution.py:155
  233.9 5.3 %select_select_fusion.1 = (bf16[32,128,512]{2,1,0:T(8,128)(2,1)}, bf16[32,128,512]{2,1,0:T(8,128)(2,1)S(1)}) fusion(bf16[32,128,512]{2,1,0:T(8,128)(2,1)} %gather_fusion.2, pred[32]{0:T(512)(128)(4,1)S(1)} %get-tuple-element.29, pred[32]{0:T(512)(128)(4,1)S(1)} %fusion.15, bf16[32,128,512]{2,1,0:T(8,128)(2,1)} %gather_fusion.3), kind=kLoop, calls=%fused_computation.15 | loop fusion | flops 8388608 | bytes 16777280 | tf_op jit(solution)/shard_map/jit(_where)/select_n | solution.py:156
  239.7 1.2 copy-done
  240.8 2.3 fusion.11
  243.2 67.9 %reduce-scatter.2.cloned.1.call-done = bf16[128,1536]{1,0:T(8,128)(2,1)} async-done(((bf16[1024,1536]{1,0:T(8,128)(2,1)}), bf16[128,1536]{1,0:T(8,128)(2,1)}) %reduce-scatter.2.cloned.1.call-update) | async-done | bytes 393232 | tf_op jit(solution)/shard_map/reduce_scatter | solution.py:59
  311.2 0.8 dynamic-slice_convert_fusion.1
  312.0 6.5 %convolution_negate_fusion = f32[512,1024]{1,0:T(8,128)} fusion(bf16[2048,1024]{1,0:T(8,128)(2,1)} %param.15, bf16[2048,1024]{1,0:T(8,128)(2,1)} %all-gather.7.cloned.1.call-done), kind=kOutput, calls=%fused_computation.21 | convolution fusion | flops 2148007936 | bytes 8388608 | tf_op jit(solution)/shard_map/dot_general | solution.py:106
  318.5 5.2 %all-to-all-start = ((f32[8,1024,64]{1,2,0:T(8,128)}), f32[8,1024,64]{1,2,0:T(8,128)}, u32[]{:S(2)}, u32[]{:S(2)}) async-start(f32[8,1024,64]{1,2,0:T(8,128)} %bitcast.23), calls=%async_computation | async-start | bytes 4194304 | tf_op jit(solution)/shard_map/all_to_all | solution.py:36
  323.6 5.0 %multiply_bitcast_fusion = f32[768,512]{0,1:T(8,128)S(1)} fusion(bf16[3072,512]{1,0:T(8,128)(2,1)S(1)} %get-tuple-element.16, bf16[3072,768]{1,0:T(8,128)(2,1)} %param.12, f32[768]{0:T(1024)S(1)} %dynamic-slice_convert_fusion.1), kind=kOutput, calls=%fused_computation.22 | convolution fusion | flops 2416705536 | bytes 9440256 | tf_op jit(solution)/shard_map/dot_general | solution.py:103
  328.7 1.1 copy-done.1
  329.9 1.5 collective-permute-start
  331.4 59.1 %collective-permute-done = f32[768,256]{0,1:T(8,128)S(1)} collective-permute-done((f32[768,256]{0,1:T(8,128)S(1)}, f32[768,256]{0,1:T(8,128)S(1)}, u32[]{:S(2)}, u32[]{:S(2)}) %collective-permute-start) | collective-permute-done | bytes 786464 | tf_op jit(solution)/shard_map/ppermute | solution.py:25
  390.5 1.5 select_add_fusion
  392.4 2.4 reduce_sum.36
  394.8 20.0 %collective-permute-done.1 = f32[768,128]{0,1:T(8,128)S(1)} collective-permute-done((f32[768,128]{0,1:T(8,128)S(1)}, f32[768,128]{0,1:T(8,128)S(1)}, u32[]{:S(2)}, u32[]{:S(2)}) %collective-permute-start.1) | collective-permute-done | bytes 393248 | tf_op jit(solution)/shard_map/ppermute | solution.py:25
  414.9 0.9 copy.12
  415.8 4.8 %fusion.28 = (bf16[16,128,512]{2,1,0:T(8,128)(2,1)}, bf16[16,128,512]{2,1,0:T(8,128)(2,1)}) fusion(bf16[32,128,512]{2,1,0:T(8,128)(2,1)} %get-tuple-element.25), kind=kLoop, calls=%fused_computation.78 | loop fusion | bytes 8388608 | tf_op jit(solution)/shard_map/slice | solution.py:161
  420.6 11.5 %fusion.6 = f32[2048,1024]{1,0:T(8,128)} fusion(bf16[1024,1536]{1,0:T(8,128)(2,1)} %all-gather.11.cloned.1.call-done, bf16[2048,512]{1,0:T(8,128)(2,1)} %bitcast.25, bf16[2048,512]{1,0:T(8,128)(2,1)} %bitcast.24, bf16[2048,512]{1,0:T(8,128)(2,1)S(1)} %copy-done.2), kind=kOutput, calls=%fused_computation.13 | convolution fusion | flops 6463422464 | bytes 17825792 | tf_op jit(solution)/shard_map/dot_general | solution.py:167
  (42 shorter events, 3.7 us)
Async XLA Ops:
  7.2 71.8 %all-gather.5.cloned.1.call-start = ((), (), s32[]{:S(2)}) async-start(), calls=%async_computation.3 | async-start | bytes 6684672 | tf_op jit(solution)/shard_map/all_gather | solution.py:15
  9.0 127.2 %all-gather.7.cloned.1.call-start = ((), (), s32[]{:S(2)}) async-start(), calls=%async_computation.4 | async-start | bytes 4456448 | tf_op jit(solution)/shard_map/all_gather | solution.py:15
  10.8 207.2 %all-gather.9.cloned.1.call-start = ((), (), s32[]{:S(2)}) async-start(), calls=%async_computation.5 | async-start | bytes 8912896 | tf_op jit(solution)/shard_map/all_gather | solution.py:15
  106.0 205.1 %reduce-scatter.2.cloned.1.call-start = ((), (), s32[]{:S(2)}) async-start(), calls=%async_computation.6 | async-start | bytes 3538944 | tf_op jit(solution)/shard_map/reduce_scatter | solution.py:59
  239.2 1.6 copy-start
  243.2 177.4 %all-gather.11.cloned.1.call-start = ((), (), s32[]{:S(2)}) async-start(), calls=%async_computation.7 | async-start | bytes 3538944 | tf_op jit(solution)/shard_map/all_gather | solution.py:60
  318.5 73.9 %all-to-all-start = ((f32[8,1024,64]{1,2,0:T(8,128)}), f32[8,1024,64]{1,2,0:T(8,128)}, u32[]{:S(2)}, u32[]{:S(2)}) async-start(f32[8,1024,64]{1,2,0:T(8,128)} %bitcast.23), calls=%async_computation | async-start | bytes 4194304 | tf_op jit(solution)/shard_map/all_to_all | solution.py:36
  328.6 1.1 copy-start.1
  329.9 60.6 %collective-permute-start = (f32[768,256]{0,1:T(8,128)S(1)}, f32[768,256]{0,1:T(8,128)S(1)}, u32[]{:S(2)}, u32[]{:S(2)}) collective-permute-start(f32[768,256]{0,1:T(8,128)S(1)} %slice_select_fusion), channel_id=1, source_target_pairs={{0,32},{32,0},{16,48},{48,16},{64,96},{96,64},{80,112},{112,80},{1... | collective-permute-start | bytes 2359304 | tf_op jit(solution)/shard_map/ppermute | solution.py:25
  392.1 22.8 %collective-permute-start.1 = (f32[768,128]{0,1:T(8,128)S(1)}, f32[768,128]{0,1:T(8,128)S(1)}, u32[]{:S(2)}, u32[]{:S(2)}) collective-permute-start(f32[768,128]{0,1:T(8,128)S(1)} %slice_select_fusion.1), channel_id=1, source_target_pairs={{0,16},{16,0},{32,48},{48,32},{64,80},{80,64},{96,112},{112,96},{1... | collective-permute-start | bytes 1179656 | tf_op jit(solution)/shard_map/ppermute | solution.py:25
  415.8 4.8 %copy-start.2 = (bf16[2048,512]{1,0:T(8,128)(2,1)S(1)}, bf16[2048,512]{1,0:T(8,128)(2,1)}, u32[]{:S(2)}) copy-start(bf16[2048,512]{1,0:T(8,128)(2,1)} %get-tuple-element.17) | copy-start | bytes 6291460
Sparse Core Ops, SparseCore 0:
  11.0 67.9 all-gather.4
  81.9 54.2 all-gather.6
  139.1 78.8 all-gather.8
  243.3 67.7 reduce-scatter.1
  312.6 98.9 all-gather.10
where the time goes:
time: 439 us
  waiting for transfers between devices  320 us (73%)
  local copies, waits for them, and re-layouts  37.1 us (8%)
  other arithmetic  24.7 us (6%)
  matrix products  23 us (5%)
  between operations  14 us (3%)
  blocking collectives  12.6 us (3%)
  starting transfers between devices  7.17 us (2%)
    all_gather x3, waiting for transfers between devices, in_one_piece(): lax.all_gather(both, axis, axis=dim, tiled=True)  173 us
    ppermute x2, waiting for transfers between devices, from_partner(): return lax.ppermute(block, axis, route)  79.1 us
    reduce_scatter x1, waiting for transfers between devices, broadcast_by_parts(): own = lax.psum_scatter(padded, axis, scatter_dimension=0, tiled=True)  67.9 us
    all_to_all x1, blocking collectives, sent_together(): lax.all_to_all(both, axis, split_axis=split_dim, concat_axis=concat_dim,...  12.6 us
    dot_general x1, matrix products, on_device(): lax.dot_general(row_side, col_side, (((1,), (1,)), ((), ())), preferred_e...  11.5 us
    split x2, local copies, waits for them, and re-layouts, in_one_piece(): jnp.split(lax.all_gather(both, axis, axis=dim, tiled=True), ends, axis=al...  10.4 us
    gather x2, local copies, waits for them, and re-layouts, place_blocks(): picked = jnp.take(received, chosen, axis=0)  9.97 us
  transfers between devices with their start and end apart: 8, of which 6 were waited for; matrix products, arithmetic and copies ran while one was open for 10% of the time, Pallas kernels for 0%

commit v1 on v0

v1 whole, which is shorter than its diff:
```python
import jax
import jax.numpy as jnp
from jax import lax
from jax.experimental import pallas as pl
from jax.experimental.pallas import tpu as pltpu
from jax.sharding import PartitionSpec as P

MESH = pl.DeviceIdType.MESH
BLK = 128
G = 8
H = 256
CAP = 4
PIECE = BLK // G
TN = (((0,), (0,)), ((), ()))
NT = (((1,), (1,)), ((), ()))
SIB = 192
PAR = 128


class Gather:
    def __init__(self, slot, own, place, at, k, major, minor, sems):
        self.slot, self.own, self.place, self.at, self.k = slot, own, place, at, k
        self.m, self.n = major, minor
        self.send, self.recv, self.chip_send, self.chip_recv, self.local = sems
        self.sent = []

    def shard(self, dm, dn):
        return lax.rem(self.m + dm, 4) * 2 + (self.n if dn == 0 else 1 - self.n)

    def push(self, src, g, to):
        i = len(self.sent)
        copy = pltpu.make_async_remote_copy(
            src_ref=src,
            dst_ref=self.slot(self.k, g),
            send_sem=self.send.at[i],
            recv_sem=self.recv.at[g],
            device_id=self.at(to),
            device_id_type=MESH,
        )
        copy.start()
        self.sent.append(copy)

    def swap(self, src, g, sibling):
        pltpu.make_async_remote_copy(
            src_ref=src,
            dst_ref=self.slot(self.k, g),
            send_sem=self.chip_send.at[g],
            recv_sem=self.chip_recv.at[g],
            device_id=sibling,
            device_id_type=MESH,
        ).start()

    def wait(self, g):
        pltpu.make_async_remote_copy(
            src_ref=self.slot(self.k, g),
            dst_ref=self.slot(self.k, g),
            send_sem=self.send.at[0],
            recv_sem=self.recv.at[g],
            device_id=self.at(self.shard(0, 0)),
            device_id_type=MESH,
        ).wait_recv()

    def start(self, sibling):
        self.sibling = sibling
        me = self.shard(0, 0)
        self.push(self.own, me, self.shard(0, 1))
        self.push(self.own, me, self.shard(1, 0))
        self.push(self.own, me, self.shard(3, 0))
        self.swap(self.own, me, sibling)
        self.place(me)

    def pair(self):
        g = self.shard(0, 1)
        self.wait(g)
        self.push(self.slot(self.k, g), g, self.shard(1, 0))
        self.push(self.slot(self.k, g), g, self.shard(3, 0))
        self.swap(self.slot(self.k, g), g, self.sibling)

    def ring(self):
        g = self.shard(1, 0)
        self.wait(g)
        self.push(self.slot(self.k, g), g, self.shard(3, 0))
        self.swap(self.slot(self.k, g), g, self.sibling)
        g = self.shard(3, 0)
        self.wait(g)
        self.swap(self.slot(self.k, g), g, self.sibling)
        g = self.shard(3, 1)
        self.wait(g)
        self.push(self.slot(self.k, g), g, self.shard(1, 0))
        self.swap(self.slot(self.k, g), g, self.sibling)

    def rest(self):
        for dm, dn in ((1, 1), (2, 0), (2, 1)):
            g = self.shard(dm, dn)
            self.wait(g)
            self.swap(self.slot(self.k, g), g, self.sibling)

    def halves(self):
        for g in range(G):
            pltpu.make_async_remote_copy(
                src_ref=self.slot(1 - self.k, g),
                dst_ref=self.slot(1 - self.k, g),
                send_sem=self.chip_send.at[g],
                recv_sem=self.chip_recv.at[g],
                device_id=self.sibling,
                device_id_type=MESH,
            ).wait_recv()

    def drain(self):
        for copy in self.sent:
            copy.wait_send()
        for g in range(G):
            pltpu.make_async_remote_copy(
                src_ref=self.slot(self.k, g),
                dst_ref=self.slot(self.k, g),
                send_sem=self.chip_send.at[g],
                recv_sem=self.chip_recv.at[g],
                device_id=self.sibling,
                device_id_type=MESH,
            ).wait_send()


def exchange_kernel(
    table,
    xin,
    sib_hbm,
    par_hbm,
    pc_out,
    lc_out,
    pp_out,
    lp_out,
    sib_out,
    parg_out,
    sib_v,
    par_v,
    sc,
    pc,
    other,
    chip_sib,
    chip_par,
    pieces,
    pack_cot,
    pack_pan,
    got_cot,
    got_pan,
    turned,
    pt,
    ct,
    far,
    near_l,
    near_r,
    zs,
    zr,
    za,
    xs,
    xa,
    ag_send,
    ag_recv,
    ag_cs,
    ag_cr,
    load_sem,
    place_sem,
    x_sem,
    b_send,
    b_recv,
    c_send,
    c_recv,
    d_send,
    d_recv,
    t_sem,
    r_send,
    r_recv,
    q_send,
    q_recv,
):
    r = lax.axis_index("row")
    c = lax.axis_index("col")
    k = c % 2
    p = c // 2
    sibling = (r, p * 2 + 1 - k)

    def in_row(q):
        return (q, c)

    def in_col(q):
        return (r, q * 2 + k)

    load_sib = pltpu.make_async_copy(sib_hbm, sib_v, load_sem.at[0])
    load_par = pltpu.make_async_copy(par_hbm, par_v, load_sem.at[1])
    load_par.start()
    load_sib.start()

    barrier = pltpu.get_barrier_semaphore()
    pl.semaphore_signal(barrier, inc=1, device_id=sibling, device_id_type=MESH)
    for d in range(1, G):
        pl.semaphore_signal(barrier, inc=1, device_id=in_row(lax.rem(r + d, G)), device_id_type=MESH)
        pl.semaphore_signal(barrier, inc=1, device_id=in_col(lax.rem(p + d, G)), device_id_type=MESH)

    @pl.when(r != p)
    def _():
        pl.semaphore_signal(barrier, inc=1, device_id=(p, r * 2 + k), device_id_type=MESH)

    pl.semaphore_wait(barrier, jnp.where(r == p, 2 * G - 1, 2 * G))

    swap = pltpu.make_async_remote_copy(
        src_ref=xin.at[1 - k],
        dst_ref=other,
        send_sem=x_sem.at[0],
        recv_sem=x_sem.at[1],
        device_id=sibling,
        device_id_type=MESH,
    )
    swap.start()
    swap.wait_recv()
    first = k == 0
    for ch in range(2):
        mine, theirs = xin[k, ch * SIB : (ch + 1) * SIB], other[ch * SIB : (ch + 1) * SIB]
        low, high = jnp.where(first, mine, theirs), jnp.where(first, theirs, mine)
        chip_sib[ch, 0] = low[:BLK]
        chip_sib[ch, 1, : BLK // 2] = low[BLK:]
        chip_sib[ch, 1, BLK // 2 :] = high[: BLK // 2]
        chip_sib[ch, 2] = high[BLK // 2 :]
        at = 2 * SIB + ch * PAR
        chip_par[ch, k] = xin[k, at : at + PAR]
        chip_par[ch, 1 - k] = other[at : at + PAR]

    def sems(i):
        return ag_send.at[i], ag_recv.at[i], ag_cs.at[i], ag_cr.at[i], place_sem.at[i]

    def place_pc(me):
        pc[k, pl.ds(me * 2, 2)] = chip_par[0]

    def place_sc(me):
        sc[k, pl.ds(me * 3, 3)] = chip_sib[0]

    def placed(src, out, i):
        def place(me):
            pltpu.make_async_copy(src, out(k, me), place_sem.at[i]).start()

        return place

    def lc_slot(h, g):
        return lc_out.at[h, g]

    def lp_slot(h, g):
        return lp_out.at[h, g]

    def pp_slot(h, g):
        return pp_out.at[h, pl.ds(g * 2, 2)]

    y, zh, x, zl = p // 2, p % 2, r // 2, r % 2
    ag_pc = Gather(lambda h, g: pc.at[h, pl.ds(g * 2, 2)], chip_par.at[0], place_pc, in_col, k, y, zh, sems(0))
    ag_sc = Gather(lambda h, g: sc.at[h, pl.ds(g * 3, 3)], chip_sib.at[0], place_sc, in_col, k, y, zh, sems(1))
    ag_lc = Gather(lc_slot, got_cot, placed(got_cot, lc_slot, 0), in_col, k, y, zh, sems(2))
    ag_lp = Gather(lp_slot, got_pan, placed(got_pan, lp_slot, 1), in_row, k, x, zl, sems(3))
    ag_pp = Gather(pp_slot, turned, placed(turned, pp_slot, 2), in_row, k, x, zl, sems(4))

    turn = pltpu.make_async_remote_copy(
        src_ref=chip_par.at[1],
        dst_ref=turned,
        send_sem=t_sem.at[0],
        recv_sem=t_sem.at[1],
        device_id=(p, r * 2 + k),
        device_id_type=MESH,
    )

    b_copies = []
    for d in range(1, G):
        to = lax.rem(p + d, G)
        copy = pltpu.make_async_remote_copy(
            src_ref=chip_sib.at[:, :, pl.ds(pl.multiple_of(to * PIECE, PIECE), PIECE)],
            dst_ref=pieces.at[:, pl.ds(p * 3, 3)],
            send_sem=b_send.at[d],
            recv_sem=b_recv.at[p],
            device_id=in_col(to),
            device_id_type=MESH,
        )
        copy.start()
        b_copies.append(copy)

    @pl.when(r != p)
    def _():
        turn.start()

    @pl.when(r == p)
    def _():
        turned[...] = chip_par[1]

    ag_pc.start(sibling)
    ag_sc.start(sibling)
    pieces[:, pl.ds(p * 3, 3)] = chip_sib[:, :, pl.ds(pl.multiple_of(p * PIECE, PIECE), PIECE)]
    for d in range(1, G):
        g = lax.rem(p + d, G)
        pltpu.make_async_remote_copy(
            src_ref=pieces.at[:, pl.ds(g * 3, 3)],
            dst_ref=pieces.at[:, pl.ds(g * 3, 3)],
            send_sem=b_send.at[d],
            recv_sem=b_recv.at[g],
            device_id=in_col(g),
            device_id_type=MESH,
        ).wait_recv()

    @pl.loop(0, G)
    def _(q):
        for t in range(CAP):
            j = table[q * CAP + t]
            pack_cot[q, t] = pieces[0, j]
            pack_pan[q, t] = pieces[1, j]

    c_copies, d_copies = [], []
    for d in range(1, G):
        to = lax.rem(p + d, G)
        copy = pltpu.make_async_remote_copy(
            src_ref=pack_pan.at[to],
            dst_ref=got_pan.at[p],
            send_sem=d_send.at[d],
            recv_sem=d_recv.at[p],
            device_id=in_col(to),
            device_id_type=MESH,
        )
        copy.start()
        d_copies.append(copy)
        to = lax.rem(r + d, G)
        copy = pltpu.make_async_remote_copy(
            src_ref=pack_cot.at[to],
            dst_ref=got_cot.at[r],
            send_sem=c_send.at[d],
            recv_sem=c_recv.at[r],
            device_id=in_row(to),
            device_id_type=MESH,
        )
        copy.start()
        c_copies.append(copy)
    got_pan[p] = pack_pan[p]
    got_cot[r] = pack_cot[r]

    @pl.when(r != p)
    def _():
        turn.wait_recv()

    ag_pp.start(sibling)
    ag_pc.pair()
    for d in range(1, G):
        g = lax.rem(p + d, G)
        pltpu.make_async_remote_copy(
            src_ref=pack_pan.at[g],
            dst_ref=got_pan.at[g],
            send_sem=d_send.at[d],
            recv_sem=d_recv.at[g],
            device_id=in_col(g),
            device_id_type=MESH,
        ).wait_recv()
    ag_lp.start(sibling)
    ag_sc.pair()
    for d in range(1, G):
        g = lax.rem(r + d, G)
        pltpu.make_async_remote_copy(
            src_ref=pack_cot.at[g],
            dst_ref=got_cot.at[g],
            send_sem=c_send.at[d],
            recv_sem=c_recv.at[g],
            device_id=in_row(g),
            device_id_type=MESH,
        ).wait_recv()
    ag_lc.start(sibling)
    ag_pc.ring()
    ag_pp.pair()
    ag_lp.pair()
    ag_lc.pair()
    ag_pc.rest()
    ag_pc.halves()
    keep_pc = pltpu.make_async_copy(pc, pc_out, place_sem.at[3])
    keep_pc.start()

    load_par.wait()
    rows_p = par_v.shape[0]

    @pl.loop(0, par_v.shape[1] // 256)
    def _(i):
        at = pl.ds(pl.multiple_of(i * 256, 256), 256)
        rhs = par_v[:, at]
        for h in range(2):
            part = lax.dot_general(
                pc[h].reshape(rows_p, H), rhs, TN, preferred_element_type=jnp.float32
            )
            pt[h * 4 : (h + 1) * 4, :, at] = part.reshape(4, H // 4, 256)

    sent = []

    def give(src, dst, i, to, s, v):
        copy = pltpu.make_async_remote_copy(
            src_ref=src, dst_ref=dst, send_sem=s.at[i], recv_sem=v.at[i], device_id=to, device_id_type=MESH
        )
        copy.start()
        sent.append(copy)

    def take(dst, i, s, v):
        pltpu.make_async_remote_copy(
            src_ref=dst, dst_ref=dst, send_sem=s.at[i], recv_sem=v.at[i], device_id=sibling, device_id_type=MESH
        ).wait_recv()

    def piece(dm, dn):
        return lax.rem(x + dm, 4) * 2 + (zl if dn == 0 else 1 - zl)

    right, left, mate = in_row(piece(1, 0)), in_row(piece(3, 0)), in_row(piece(0, 1))
    give(pt.at[piece(2, 0)], far.at[0], 0, right, r_send, r_recv)
    give(pt.at[piece(2, 1)], far.at[1], 1, left, r_send, r_recv)
    give(pt.at[piece(1, 1)], near_l.at[1], 2, right, r_send, r_recv)
    give(pt.at[piece(3, 0)], near_r.at[0], 3, left, r_send, r_recv)

    ag_sc.ring()
    ag_pp.ring()
    ag_lp.ring()
    ag_lc.ring()
    ag_sc.rest()
    take(far.at[0], 0, r_send, r_recv)
    pt[piece(1, 0)] = pt[piece(1, 0)] + far[0]
    give(pt.at[piece(1, 0)], near_l.at[0], 4, right, r_send, r_recv)
    take(far.at[1], 1, r_send, r_recv)
    pt[piece(3, 1)] = pt[piece(3, 1)] + far[1]
    give(pt.at[piece(3, 1)], near_r.at[1], 5, left, r_send, r_recv)
    ag_sc.halves()

    load_sib.wait()
    rows_s = sib_v.shape[0]

    @pl.loop(0, sib_v.shape[1] // 256)
    def _(i):
        at = pl.ds(pl.multiple_of(i * 256, 256), 256)
        rhs = sib_v[:, at]
        for h in range(2):
            part = lax.dot_general(
                sc[h].reshape(rows_s, H), rhs, TN, preferred_element_type=jnp.float32
            )
            ct[h * 2 : (h + 1) * 2, :, at] = part.reshape(2, H // 2, 256)

    xb = x % 2
    beside = in_row((x + 1 - 2 * xb) * 2 + zl)
    give(ct.at[(1 - xb) * 2 + 1 - zl], za.at[1], 0, mate, q_send, q_recv)
    give(ct.at[xb * 2 + 1 - zl], za.at[0], 1, mate, q_send, q_recv)

    take(near_l.at[1], 2, r_send, r_recv)
    take(near_r.at[1], 5, r_send, r_recv)
    zs[...] = pt[piece(0, 1)] + near_l[1] + near_r[1]
    give(zs, zr, 6, mate, r_send, r_recv)

    take(za.at[1], 0, q_send, q_recv)
    xs[...] = ct[(1 - xb) * 2 + zl] + za[1]
    give(xs, xa, 2, beside, q_send, q_recv)

    ag_pp.rest()
    ag_lp.rest()
    ag_lc.rest()

    take(near_l.at[0], 4, r_send, r_recv)
    take(near_r.at[0], 3, r_send, r_recv)
    take(zr, 6, r_send, r_recv)
    parg_out[...] = pt[piece(0, 0)] + near_l[0] + near_r[0] + zr[...]
    take(za.at[0], 1, q_send, q_recv)
    take(xa, 2, q_send, q_recv)
    sib_out[...] = ct[xb * 2 + zl] + za[0] + xa[...]

    ag_pp.halves()
    ag_lp.halves()
    ag_lc.halves()

    swap.wait_send()

    @pl.when(r != p)
    def _():
        turn.wait_send()

    for copy in b_copies + c_copies + d_copies + sent:
        copy.wait_send()
    for ag in (ag_pc, ag_sc, ag_lc, ag_lp, ag_pp):
        ag.drain()
    pltpu.make_async_copy(got_cot, lc_slot(k, p), place_sem.at[0]).wait()
    pltpu.make_async_copy(got_pan, lp_slot(k, r), place_sem.at[1]).wait()
    pltpu.make_async_copy(turned, pp_slot(k, r), place_sem.at[2]).wait()
    keep_pc.wait()


def exchange(table, xin, sib_inverse, par_inverse):
    bf, f32 = jnp.bfloat16, jnp.float32
    srows, scols = sib_inverse.shape
    prows, pcols = par_inverse.shape
    anyspace = pl.BlockSpec(memory_space=pl.ANY)
    vmem = pl.BlockSpec(memory_space=pltpu.VMEM)
    dma = pltpu.SemaphoreType.DMA
    lifted = (2, G, G, CAP, PIECE, H)
    return pl.pallas_call(
        exchange_kernel,
        out_shape=(
            jax.ShapeDtypeStruct((2, 2 * G, BLK, H), bf),
            jax.ShapeDtypeStruct(lifted, bf),
            jax.ShapeDtypeStruct((2, 2 * G, BLK, H), bf),
            jax.ShapeDtypeStruct(lifted, bf),
            jax.ShapeDtypeStruct((H // 2, scols), f32),
            jax.ShapeDtypeStruct((H // 4, pcols), f32),
        ),
        in_specs=[pl.BlockSpec(memory_space=pltpu.SMEM), vmem, anyspace, anyspace],
        out_specs=(anyspace, anyspace, anyspace, anyspace, vmem, vmem),
        scratch_shapes=[
            pltpu.VMEM((srows, scols), bf),
            pltpu.VMEM((prows, pcols), bf),
            pltpu.VMEM((2, 3 * G, BLK, H), bf),
            pltpu.VMEM((2, 2 * G, BLK, H), bf),
            pltpu.VMEM((2 * (SIB + PAR), H), bf),
            pltpu.VMEM((2, 3, BLK, H), bf),
            pltpu.VMEM((2, 2, BLK, H), bf),
            pltpu.VMEM((2, 3 * G, PIECE, H), bf),
            pltpu.VMEM((G, CAP, PIECE, H), bf),
            pltpu.VMEM((G, CAP, PIECE, H), bf),
            pltpu.VMEM((G, CAP, PIECE, H), bf),
            pltpu.VMEM((G, CAP, PIECE, H), bf),
            pltpu.VMEM((2, BLK, H), bf),
            pltpu.VMEM((8, H // 4, pcols), f32),
            pltpu.VMEM((4, H // 2, scols), f32),
            pltpu.VMEM((2, H // 4, pcols), f32),
            pltpu.VMEM((2, H // 4, pcols), f32),
            pltpu.VMEM((2, H // 4, pcols), f32),
            pltpu.VMEM((H // 4, pcols), f32),
            pltpu.VMEM((H // 4, pcols), f32),
            pltpu.VMEM((2, H // 2, scols), f32),
            pltpu.VMEM((H // 2, scols), f32),
            pltpu.VMEM((H // 2, scols), f32),
            dma((5, 8)),
            dma((5, 8)),
            dma((5, 8)),
            dma((5, 8)),
            dma((2,)),
            dma((5,)),
            dma((2,)),
            dma((8,)),
            dma((8,)),
            dma((8,)),
            dma((8,)),
            dma((8,)),
            dma((8,)),
            dma((2,)),
            dma((7,)),
            dma((7,)),
            dma((3,)),
            dma((3,)),
        ],
        compiler_params=pltpu.CompilerParams(
            collective_id=0, has_side_effects=True, vmem_limit_bytes=50 << 20
        ),
    )(table, xin, sib_inverse, par_inverse)


def border_kernel(row_tab, col_tab, pc, a00, a01, a10, a11, pp, lp, out, left, right):
    i = pl.program_id(0)

    @pl.when(i == 0)
    def _():
        for b in range(8):
            rows = slice(b * BLK, (b + 1) * BLK)
            for h in range(2):
                right[rows, h * H : (h + 1) * H] = pp[h, b]
            for s in range(2):
                slot = col_tab[s * 8 + b]
                live = slot >= 0
                at = jnp.maximum(slot, 0)
                for h in range(2):
                    lanes = slice((1 + s) * 2 * H + h * H, (1 + s) * 2 * H + (h + 1) * H)
                    block = lp[h, at // CAP, :, at % CAP].reshape(BLK, H)
                    right[rows, lanes] = jnp.where(live, block, jnp.zeros_like(block))

    for b in range(2):
        rows = slice(b * BLK, (b + 1) * BLK)
        for h in range(2):
            left[rows, h * H : (h + 1) * H] = pc[h, b]
        for s, ref in enumerate(((a00, a01)[b], (a10, a11)[b])):
            live = row_tab[s * 16 + i * 2 + b] >= 0
            for h in range(2):
                lanes = slice((1 + s) * 2 * H + h * H, (1 + s) * 2 * H + (h + 1) * H)
                block = ref[h, :, 0].reshape(BLK, H)
                left[rows, lanes] = jnp.where(live, block, jnp.zeros_like(block))
    out[...] = lax.dot_general(left[...], right[...], NT, preferred_element_type=jnp.float32)


def border(row_tab, col_tab, half, pc, lc, pp, lp):
    rows = 2 * G * BLK
    cols = G * BLK
    lc = lc.reshape(2, G, G * CAP, PIECE, H)

    def slot_spec(s, b):
        return pl.BlockSpec(
            (2, G, 1, PIECE, H),
            lambda i, rt, ct, hf: (0, 0, jnp.maximum(rt[s * 16 + i * 2 + b], 0), 0, 0),
        )

    def body(rt, ct, hf, *refs):
        border_kernel(rt, ct, *refs)

    return pl.pallas_call(
        body,
        out_shape=jax.ShapeDtypeStruct((rows, cols), jnp.float32),
        grid_spec=pltpu.PrefetchScalarGridSpec(
            num_scalar_prefetch=3,
            grid=(G,),
            in_specs=[
                pl.BlockSpec((2, 2, BLK, H), lambda i, rt, ct, hf: (0, i, 0, 0)),
                slot_spec(0, 0),
                slot_spec(0, 1),
                slot_spec(1, 0),
                slot_spec(1, 1),
                pl.BlockSpec((2, 8, BLK, H), lambda i, rt, ct, hf: (0, hf[0], 0, 0)),
                pl.BlockSpec((2, G, G, CAP, PIECE, H), lambda i, rt, ct, hf: (0, 0, 0, 0, 0, 0)),
            ],
            out_specs=pl.BlockSpec((2 * BLK, cols), lambda i, rt, ct, hf: (i, 0)),
            scratch_shapes=[
                pltpu.VMEM((2 * BLK, 6 * H), jnp.bfloat16),
                pltpu.VMEM((cols, 6 * H), jnp.bfloat16),
            ],
        ),
        compiler_params=pltpu.CompilerParams(vmem_limit_bytes=50 << 20),
    )(row_tab, col_tab, half, pc, lc, lc, lc, lc, pp, lp)


def on_device(sib_inverse, sib_panel, sib_cot, par_inverse, par_panel, par_cot, block_map, row_mask):
    r = lax.axis_index("row")
    c = lax.axis_index("col")
    tile_cols = sib_inverse.shape[1]
    half_rows = G // 2
    tile_blocks = 3 * G
    parent_blocks = 2 * G

    live = lax.dynamic_slice_in_dim(row_mask, (r * 16 + c) * SIB, SIB).astype(jnp.bfloat16)[:, None]
    xin = jnp.concatenate([sib_cot * live, -(sib_panel * live), par_cot, -par_panel], axis=0)
    xin = xin.reshape(-1, 2, H).transpose(1, 0, 2)

    ids = block_map.reshape(G, tile_blocks)
    dest = ids // parent_blocks
    iota = jnp.arange(tile_blocks, dtype=jnp.int32)
    before = (dest[:, :, None] == dest[:, None, :]) & (iota[None, None, :] < iota[None, :, None])
    rank = jnp.sum(before.astype(jnp.int32), axis=-1)
    mine = lax.dynamic_index_in_dim(dest * CAP + rank, r, 0, keepdims=False)
    slots = jnp.arange(G * CAP, dtype=jnp.int32)
    table = jnp.sum(jnp.where(mine[None, :] == slots[:, None], iota[None, :], 0), axis=1)

    held = (jnp.arange(G, dtype=jnp.int32)[:, None] * CAP + rank).reshape(2, -1)
    flat = block_map.reshape(2, -1)

    def lookup(first, count):
        want = first + jnp.arange(count, dtype=jnp.int32)
        hit = flat[:, None, :] == want[None, :, None]
        return (jnp.sum(jnp.where(hit, held[:, None, :] + 1, 0), axis=-1) - 1).reshape(-1)

    row_tab = lookup(r * parent_blocks, parent_blocks)
    col_tab = lookup(c * G, G)

    pc, lc, pp, lp, sib_sum, par_sum = exchange(table, xin, sib_inverse, par_inverse)
    border_grad = border(row_tab, col_tab, (c % 2).reshape(1), pc, lc, pp, lp)

    live_cols = lax.dynamic_slice_in_dim(
        row_mask, (r // half_rows) * (tile_cols * 16) + c * tile_cols, tile_cols
    ).astype(jnp.float32)
    return (-(sib_sum * live_cols[None, :]).T, -par_sum.T, border_grad)


def solution(mesh):
    placed = (
        P("row", "col"),
        P(("row", "col"), None),
        P(("row", "col"), None),
        P("row", "col"),
        P(("row", "col"), None),
        P(("row", "col"), None),
        P(),
        P(),
    )
    return jax.shard_map(
        on_device,
        mesh=mesh,
        in_specs=placed,
        out_specs=(P("col", "row"), P("col", "row"), P("row", "col")),
        check_vma=False,
    )
```

time: 439 us -> 118 us (0.27)
  waiting for transfers between devices: 320 us -> 0 us
  Pallas kernels: 0 us -> 107 us
  local copies, waits for them, and re-layouts: 37.1 us -> 2.62 us
  matrix products: 23 us -> 0 us
  other arithmetic: 24.7 us -> 7.47 us
  between operations: 14 us -> 0.74 us
  blocking collectives: 12.6 us -> 0 us
  starting transfers between devices: 7.17 us -> 0 us
    all_gather x4 -> x0, waiting for transfers between devices: 173 us -> none  [the longest x3 173 us: in_one_piece(): lax.all_gather(both, axis, axis=dim, tiled=True)]
    pallas_call x0 -> x2, Pallas kernels: none -> 107 us  [the longest x1 92.6 us: exchange(): pl.pallas_call(exchange_kernel, out_shape=(jax.ShapeDtypeStruct((2, 2 * G...]
    ppermute x2 -> x0, waiting for transfers between devices: 79.1 us -> none  [from_partner(): return lax.ppermute(block, axis, route)]
    reduce_scatter x1 -> x0, waiting for transfers between devices: 67.9 us -> none  [broadcast_by_parts(): own = lax.psum_scatter(padded, axis, scatter_dimension=0, tiled=True)]
    dot_general x3 -> x0, matrix products: 23 us -> none  [the longest x1 11.5 us: on_device(): lax.dot_general(row_side, col_side, (((1,), (1,)), ((), ())), preferred_e...]
    gather x4 -> x0, local copies, waits for them, and re-layouts: 17.5 us -> none  [the longest x2 9.97 us: place_blocks(): picked = jnp.take(received, chosen, axis=0)]
    all_to_all x1 -> x0, blocking collectives: 12.6 us -> none  [sent_together(): lax.all_to_all(both, axis, split_axis=split_dim, concat_axis=concat_dim,...]
    split x3 -> x0, local copies, waits for them, and re-layouts: 10.4 us -> none  [the longest x2 10.4 us: in_one_piece(): jnp.split(lax.all_gather(both, axis, axis=dim, tiled=True), ends, axis=al...]
  transfers between devices with their start and end apart: 8 -> 0, of which waited for: 6 -> 0; matrix products, arithmetic and copies ran while one was open for 10% -> 0% of each run, Pallas kernels for 0% -> 0%
where the time goes in v1:
time: 118 us
  Pallas kernels  107 us (91%)
  other arithmetic  7.47 us (6%)
  local copies, waits for them, and re-layouts  2.62 us (2%)
    pallas_call x1, Pallas kernels, exchange(): pl.pallas_call(exchange_kernel, out_shape=(jax.ShapeDtypeStruct((2, 2 * G...  92.6 us
    pallas_call x1, Pallas kernels, border(): pl.pallas_call(body, out_shape=jax.ShapeDtypeStruct((rows, cols), jnp.flo...  14.3 us

profile of v1, /device:TPU:1, one launch (start us, length us, event | category | flops | bytes accessed | tf_op | source)
XLA Modules:
  0.0 117.7 jit_solution(1103218652177526344)
XLA Ops:
  0.7 0.8 dynamic-slice_convert_fusion.1
  1.5 0.1 add.92
  1.5 0.1 add.93
  1.6 0.8 dynamic-slice_convert_fusion
  2.4 0.8 reshape.129
  3.2 0.3 convert_reduce_fusion
  3.5 0.1 reduce_sum.40
  3.6 0.1 select_reduce_fusion.1.table
  3.7 0.9 select_reduce_fusion.2
  4.5 0.9 select_reduce_fusion
  5.4 0.1 sub.24.rt
  5.5 0.1 sub.26.ct
  5.6 0.9 neg.19
  6.5 1.1 broadcast_multiply_fusion
  7.6 1.0 pad_maximum_fusion
  8.6 0.3 copy.24
  8.9 0.2 copy.25
  9.1 92.6 %shard_map.103 = (bf16[2,16,128,256]{3,2,1,0:T(8,128)(2,1)S(1)}, bf16[2,8,8,4,16,256]{5,4,3,2,1,0:T(8,128)(2,1)}, bf16[2,16,128,256]{3,2,1,0:T(8,128)(2,1)}, bf1...) custom-call(s32[32]{0:T(128)S(1)} %select_reduce_fusion.1.table, ...), custom_call_target="tpu_custom_call" | custom-call | tf_op jit(solution)/shard_map/pallas_call | solution.py:491
  101.8 0.9 copy.26
  102.7 0.7 negate_bitcast_fusion.1
  103.4 14.3 %shard_map.104 = f32[2048,1024]{1,0:T(8,128)} custom-call(s32[32]{0:T(128)S(1)} %sub.24.rt, s32[16]{0:T(128)S(1)} %sub.26.ct, s32[1]{0:T(128)} %bitcast.5.hf, bf16[2,16,128,256]{3,2,1,0:T(8,128)(2,1)S(1)} %get-tuple-element.11.refs_0_, bf16[2,8,32,16,256]{4,3,2,1,0:T(8,128)(2,1)} %bitcast.11, bf16[2,8,32,16,256]{4,3,2,1,0:T(8,128)(2,1)} %bitcast.12, ...), custom_call_target="tpu_custom_call" | custom-call | tf_op jit(solution)/shard_map/pallas_call | solution.py:597
  (11 shorter events, 0.1 us)

commit v2 on v1

v2 whole, which is shorter than its diff:
```python
import jax
import jax.numpy as jnp
from jax import lax
from jax.experimental import pallas as pl
from jax.experimental.pallas import tpu as pltpu
from jax.sharding import PartitionSpec as P

MESH = pl.DeviceIdType.MESH
BLK = 128
G = 8
H = 256
CAP = 4
PIECE = BLK // G
TN = (((0,), (0,)), ((), ()))
NT = (((1,), (1,)), ((), ()))
SIB = 192
PAR = 128
ROW_TAB, COL_TAB, END = 32, 64, 80


class Gather:
    def __init__(self, slot, own, place, at, k, major, minor, sems):
        self.slot, self.own, self.place, self.at, self.k = slot, own, place, at, k
        self.m, self.n = major, minor
        self.send, self.recv, self.chip_send, self.chip_recv = sems
        self.sent = []

    def shard(self, dm, dn):
        return lax.rem(self.m + dm, 4) * 2 + (self.n if dn == 0 else 1 - self.n)

    def push(self, src, g, to):
        i = len(self.sent)
        copy = pltpu.make_async_remote_copy(
            src_ref=src,
            dst_ref=self.slot(self.k, g),
            send_sem=self.send.at[i],
            recv_sem=self.recv.at[g],
            device_id=self.at(to),
            device_id_type=MESH,
        )
        copy.start()
        self.sent.append(copy)

    def swap(self, src, g, sibling):
        pltpu.make_async_remote_copy(
            src_ref=src,
            dst_ref=self.slot(self.k, g),
            send_sem=self.chip_send.at[g],
            recv_sem=self.chip_recv.at[g],
            device_id=sibling,
            device_id_type=MESH,
        ).start()

    def wait(self, g):
        pltpu.make_async_remote_copy(
            src_ref=self.slot(self.k, g),
            dst_ref=self.slot(self.k, g),
            send_sem=self.send.at[0],
            recv_sem=self.recv.at[g],
            device_id=self.at(self.shard(0, 0)),
            device_id_type=MESH,
        ).wait_recv()

    def start(self, sibling):
        self.sibling = sibling
        me = self.shard(0, 0)
        self.push(self.own, me, self.shard(0, 1))
        self.push(self.own, me, self.shard(1, 0))
        self.push(self.own, me, self.shard(3, 0))
        self.swap(self.own, me, sibling)
        self.place(me)

    def pair(self):
        g = self.shard(0, 1)
        self.wait(g)
        self.push(self.slot(self.k, g), g, self.shard(1, 0))
        self.push(self.slot(self.k, g), g, self.shard(3, 0))
        self.swap(self.slot(self.k, g), g, self.sibling)

    def ring(self):
        g = self.shard(1, 0)
        self.wait(g)
        self.push(self.slot(self.k, g), g, self.shard(3, 0))
        self.swap(self.slot(self.k, g), g, self.sibling)
        g = self.shard(3, 0)
        self.wait(g)
        self.swap(self.slot(self.k, g), g, self.sibling)
        g = self.shard(3, 1)
        self.wait(g)
        self.push(self.slot(self.k, g), g, self.shard(1, 0))
        self.swap(self.slot(self.k, g), g, self.sibling)

    def rest(self):
        for dm, dn in ((1, 1), (2, 0), (2, 1)):
            g = self.shard(dm, dn)
            self.wait(g)
            self.swap(self.slot(self.k, g), g, self.sibling)

    def halves(self):
        for g in range(G):
            pltpu.make_async_remote_copy(
                src_ref=self.slot(1 - self.k, g),
                dst_ref=self.slot(1 - self.k, g),
                send_sem=self.chip_send.at[g],
                recv_sem=self.chip_recv.at[g],
                device_id=self.sibling,
                device_id_type=MESH,
            ).wait_recv()

    def drain(self):
        for copy in self.sent:
            copy.wait_send()
        for g in range(G):
            pltpu.make_async_remote_copy(
                src_ref=self.slot(self.k, g),
                dst_ref=self.slot(self.k, g),
                send_sem=self.chip_send.at[g],
                recv_sem=self.chip_recv.at[g],
                device_id=self.sibling,
                device_id_type=MESH,
            ).wait_send()


STEP = 4


def exchange_kernel(
    tab,
    mask_hbm,
    sib_cot_hbm,
    sib_panel_hbm,
    par_cot_hbm,
    par_panel_hbm,
    sib_hbm,
    par_hbm,
    part_out,
    lc_out,
    lp_out,
    sib_out,
    parg_out,
    mask,
    sib_cot,
    sib_panel,
    par_panel,
    sib_v,
    par_v,
    sc,
    pc,
    pp,
    mcol,
    halves,
    other,
    halves_p,
    other_p,
    chip_sib,
    chip_par,
    pieces,
    par_pieces,
    pack_cot,
    pack_pan,
    got_cot,
    got_pan,
    got_par,
    pt,
    ct,
    far,
    near_l,
    near_r,
    zs,
    zr,
    s_in,
    s_mid,
    s_last,
    pmat,
    tiles,
    ag_send,
    ag_recv,
    ag_cs,
    ag_cr,
    load_sem,
    place_sem,
    tile_sem,
    x_sem,
    b_send,
    b_recv,
    e_send,
    e_recv,
    c_send,
    c_recv,
    d_send,
    d_recv,
    f_send,
    f_recv,
    r_send,
    r_recv,
    q_send,
    q_recv,
):
    r = lax.axis_index("row")
    c = lax.axis_index("col")
    k = c % 2
    p = c // 2
    y, zh, x, zl = p // 2, p % 2, r // 2, r % 2
    sibling = (r, p * 2 + 1 - k)
    started = []

    def in_row(q):
        return (q, c)

    def in_col(q):
        return (r, q * 2 + k)

    def remote(src, dst, send, recv, to):
        return pltpu.make_async_remote_copy(
            src_ref=src, dst_ref=dst, send_sem=send, recv_sem=recv, device_id=to, device_id_type=MESH
        )

    def give(src, dst, send, recv, to):
        copy = remote(src, dst, send, recv, to)
        copy.start()
        started.append(copy)

    def take(dst, send, recv):
        remote(dst, dst, send, recv, sibling).wait_recv()

    def each(dst, at, me, send, recv):
        for d in range(1, G):
            g = lax.rem(me + d, G)
            take(dst.at[at(g)], send.at[d], recv.at[g])

    barrier = pltpu.get_barrier_semaphore()
    pl.semaphore_signal(barrier, inc=1, device_id=sibling, device_id_type=MESH)
    for d in range(1, G):
        pl.semaphore_signal(barrier, inc=1, device_id=in_row(lax.rem(r + d, G)), device_id_type=MESH)
        pl.semaphore_signal(barrier, inc=1, device_id=in_col(lax.rem(p + d, G)), device_id_type=MESH)
    loads = [
        pltpu.make_async_copy(src, dst, load_sem.at[i])
        for i, (src, dst) in enumerate(
            (
                (par_panel_hbm, par_panel),
                (par_cot_hbm, pc.at[c]),
                (mask_hbm, mask),
                (sib_cot_hbm, sib_cot),
                (sib_panel_hbm, sib_panel),
                (par_hbm, par_v),
                (sib_hbm, sib_v),
            )
        )
    ]
    for load in loads:
        load.start()

    def sems(i):
        return ag_send.at[i], ag_recv.at[i], ag_cs.at[i], ag_cr.at[i]

    def nothing(me):
        pass

    def placed(src, out, i):
        def place(me):
            pltpu.make_async_copy(src, out(k, me), place_sem.at[i]).start()

        return place

    def place_pp(me):
        pp[k, me] = got_par[...]

    def lc_slot(h, g):
        return lc_out.at[h, g]

    def lp_slot(h, g):
        return lp_out.at[h, g]

    ag_pc = Gather(lambda h, g: pc.at[g * 2 + h], pc.at[c], nothing, in_col, k, y, zh, sems(0))
    ag_sc = Gather(lambda h, g: sc.at[g * 2 + h], sc.at[c], nothing, in_col, k, y, zh, sems(1))
    ag_lc = Gather(lc_slot, got_cot, placed(got_cot, lc_slot, 0), in_col, k, y, zh, sems(2))
    ag_lp = Gather(lp_slot, got_pan, placed(got_pan, lp_slot, 1), in_row, k, x, zl, sems(3))
    ag_pp = Gather(lambda h, g: pp.at[h, g], got_par, place_pp, in_row, k, x, zl, sems(4))

    loads[0].wait()
    for h in range(2):
        halves_p[h] = par_panel[:, h * H : (h + 1) * H]
    loads[1].wait()
    pl.semaphore_wait(barrier, 2 * G - 1)
    give(halves_p.at[1 - k], other_p, x_sem.at[0], x_sem.at[1], sibling)
    ag_pc.start(sibling)

    for load in loads[2:5]:
        load.wait()
    line = (r * 16 + c) * 3 // 2
    for i in range(2):
        row = mask[pl.ds(line + i, 1), :].astype(jnp.float32)
        mcol[i * BLK : (i + 1) * BLK] = jnp.broadcast_to(row, (BLK, BLK)).T.astype(jnp.bfloat16)
    live = mcol[pl.ds(pl.multiple_of(k * 64, 64), SIB)]
    for h in range(2):
        for i in range(2):
            lanes = slice(h * H + i * BLK, h * H + (i + 1) * BLK)
            cot = sib_cot[:, lanes] * live
            sc[c, :, lanes] = cot
            halves[h, :SIB, i * BLK : (i + 1) * BLK] = cot
            halves[h, SIB:, i * BLK : (i + 1) * BLK] = sib_panel[:, lanes] * live
    give(halves.at[1 - k], other, x_sem.at[2], x_sem.at[3], sibling)

    def strip(i):
        return pl.ds(pl.multiple_of(i * PIECE, PIECE), PIECE)

    take(other_p, x_sem.at[0], x_sem.at[1])
    chip_par[k] = halves_p[k]
    chip_par[1 - k] = other_p[...]
    for d in range(1, G):
        to = lax.rem(r + d, G)
        give(chip_par.at[:, strip(to)], par_pieces.at[r], e_send.at[d], e_recv.at[r], in_row(to))
    par_pieces[r] = chip_par[:, strip(r)]

    take(other, x_sem.at[2], x_sem.at[3])
    first = k == 0
    for ch in range(2):
        mine, theirs = halves[k, ch * SIB : (ch + 1) * SIB], other[ch * SIB : (ch + 1) * SIB]
        low, high = jnp.where(first, mine, theirs), jnp.where(first, theirs, mine)
        chip_sib[ch, 0] = low[:BLK]
        chip_sib[ch, 1, : BLK // 2] = low[BLK:]
        chip_sib[ch, 1, BLK // 2 :] = high[: BLK // 2]
        chip_sib[ch, 2] = high[BLK // 2 :]
    for d in range(1, G):
        to = lax.rem(p + d, G)
        give(chip_sib.at[:, :, strip(to)], pieces.at[:, pl.ds(p * 3, 3)], b_send.at[d], b_recv.at[p], in_col(to))
    pieces[:, pl.ds(p * 3, 3)] = chip_sib[:, :, strip(p)]

    each(par_pieces, lambda g: g, r, e_send, e_recv)
    for d in range(1, G):
        to = lax.rem(p + d, G)
        give(par_pieces.at[to], got_par.at[p], f_send.at[d], f_recv.at[p], in_col(to))
    got_par[p] = par_pieces[p]

    ag_pc.pair()
    for d in range(1, G):
        g = lax.rem(p + d, G)
        take(pieces.at[:, pl.ds(g * 3, 3)], b_send.at[d], b_recv.at[g])

    @pl.loop(0, G)
    def _(q):
        for t in range(CAP):
            j = tab[q * CAP + t]
            pack_cot[q, t] = pieces[0, j]
            pack_pan[q, t] = pieces[1, j]

    for d in range(1, G):
        to = lax.rem(p + d, G)
        give(pack_pan.at[to], got_pan.at[p], d_send.at[d], d_recv.at[p], in_col(to))
    for d in range(1, G):
        to = lax.rem(r + d, G)
        give(pack_cot.at[to], got_cot.at[r], c_send.at[d], c_recv.at[r], in_row(to))
    got_pan[p] = pack_pan[p]
    got_cot[r] = pack_cot[r]

    each(got_par, lambda g: g, p, f_send, f_recv)
    ag_pp.start(sibling)
    ag_pc.ring()
    each(got_pan, lambda g: g, p, d_send, d_recv)
    ag_lp.start(sibling)
    each(got_cot, lambda g: g, r, c_send, c_recv)
    ag_lc.start(sibling)
    ag_pc.rest()
    ag_pp.pair()
    ag_pc.halves()

    loads[5].wait()
    rows_p = par_v.shape[0]

    @pl.loop(0, par_v.shape[1] // 256)
    def _(i):
        at = pl.ds(pl.multiple_of(i * 256, 256), 256)
        part = lax.dot_general(
            pc[...].reshape(rows_p, 2 * H), par_v[:, at], TN, preferred_element_type=jnp.float32
        )
        pt[:, :, at] = part.reshape(8, H // 4, 256)

    def piece(dm, dn):
        return lax.rem(x + dm, 4) * 2 + (zl if dn == 0 else 1 - zl)

    right, left, mate = in_row(piece(1, 0)), in_row(piece(3, 0)), in_row(piece(0, 1))

    def r_give(src, dst, i, to):
        give(src, dst, r_send.at[i], r_recv.at[i], to)

    def r_take(dst, i):
        take(dst, r_send.at[i], r_recv.at[i])

    def q_give(src, dst, i, to):
        give(src, dst, q_send.at[i], q_recv.at[i], to)

    def q_take(dst, i):
        take(dst, q_send.at[i], q_recv.at[i])

    r_give(pt.at[piece(2, 0)], far.at[0], 0, right)
    r_give(pt.at[piece(2, 1)], far.at[1], 1, left)
    r_give(pt.at[piece(1, 1)], near_l.at[1], 2, right)
    r_give(pt.at[piece(3, 0)], near_r.at[0], 3, left)

    ag_sc.start(sibling)
    ag_lp.pair()
    ag_lc.pair()
    ag_pp.ring()
    ag_sc.pair()

    r_take(far.at[0], 0)
    pt[piece(1, 0)] = pt[piece(1, 0)] + far[0]
    r_give(pt.at[piece(1, 0)], near_l.at[0], 4, right)
    r_take(far.at[1], 1)
    pt[piece(3, 1)] = pt[piece(3, 1)] + far[1]
    r_give(pt.at[piece(3, 1)], near_r.at[1], 5, left)

    ag_sc.ring()
    ag_lc.ring()
    ag_sc.rest()
    ag_sc.halves()

    loads[6].wait()
    rows_s, cols_s = sib_v.shape
    cut = cols_s // 3 * 2
    parts = (slice(0, cut), slice(cut, cols_s))
    xb = x % 2
    beside = in_row((x + 1 - 2 * xb) * 2 + zl)
    own, by_z, by_x, by_xz = xb * 2 + zl, xb * 2 + 1 - zl, (1 - xb) * 2 + zl, (1 - xb) * 2 + 1 - zl

    def sib_part(i):
        part = lax.dot_general(
            sc[...].reshape(rows_s, 2 * H), sib_v[:, parts[i]], TN, preferred_element_type=jnp.float32
        )
        ct[:, :, parts[i]] = part.reshape(4, H // 2, -1)

    sib_part(0)
    q_give(ct.at[by_xz, :, parts[0]], s_in.at[1, :, parts[0]], 0, mate)
    q_give(ct.at[by_z, :, parts[0]], s_in.at[0, :, parts[0]], 1, mate)
    sib_part(1)
    q_give(ct.at[by_xz, :, parts[1]], s_in.at[1, :, parts[1]], 2, beside)
    q_give(ct.at[by_x, :, parts[1]], s_in.at[0, :, parts[1]], 3, beside)

    ag_lp.ring()
    ag_pp.rest()

    r_take(near_l.at[1], 2)
    r_take(near_r.at[1], 5)
    zs[...] = pt[piece(0, 1)] + near_l[1] + near_r[1]
    r_give(zs, zr, 6, mate)

    ag_pp.halves()
    for n in range(8):
        rows = slice(n * BLK, (n + 1) * BLK)
        for h in range(2):
            pmat[rows, h * H : (h + 1) * H] = pp[h, :, 4 * k + n // 2, n % 2].reshape(BLK, H)
    rows_t = STEP * BLK
    stores = []

    def tile(t):
        if t >= 2:
            stores[t - 2].wait()
        tiles[t % 2] = lax.dot_general(
            pc[t * STEP : (t + 1) * STEP].reshape(rows_t, 2 * H),
            pmat[...],
            NT,
            preferred_element_type=jnp.float32,
        )
        stores.append(
            pltpu.make_async_copy(tiles.at[t % 2], part_out.at[t * rows_t : (t + 1) * rows_t], tile_sem.at[t % 2])
        )
        stores[t].start()

    tile(0)
    q_take(s_in.at[1, :, parts[1]], 2)
    s_mid[:, parts[1]] = ct[by_z, :, parts[1]] + s_in[1, :, parts[1]]
    q_give(s_mid.at[:, parts[1]], s_last.at[:, parts[1]], 5, mate)
    tile(1)
    q_take(s_in.at[1, :, parts[0]], 0)
    s_mid[:, parts[0]] = ct[by_x, :, parts[0]] + s_in[1, :, parts[0]]
    q_give(s_mid.at[:, parts[0]], s_last.at[:, parts[0]], 4, beside)
    tile(2)
    ag_lc.rest()
    ag_lp.rest()
    tile(3)

    r_take(near_l.at[0], 4)
    r_take(near_r.at[0], 3)
    r_take(zr, 6)
    parg_out[...] = -(pt[piece(0, 0)] + near_l[0] + near_r[0] + zr[...])
    q_take(s_in.at[0, :, parts[0]], 1)
    q_take(s_in.at[0, :, parts[1]], 3)
    q_take(s_last.at[:, parts[0]], 4)
    q_take(s_last.at[:, parts[1]], 5)
    first_line = (x // 2) * (mask.shape[0] // 2) + c * (cols_s // BLK)
    for j in range(cols_s // BLK):
        lanes = slice(j * BLK, (j + 1) * BLK)
        keep = mask[pl.ds(first_line + j, 1), :].astype(jnp.float32)
        sib_out[:, lanes] = -(ct[own, :, lanes] + s_in[0, :, lanes] + s_last[:, lanes]) * keep

    ag_lc.halves()
    ag_lp.halves()

    for copy in started:
        copy.wait_send()
    for ag in (ag_pc, ag_sc, ag_lc, ag_lp, ag_pp):
        ag.drain()
    pltpu.make_async_copy(got_cot, lc_slot(k, p), place_sem.at[0]).wait()
    pltpu.make_async_copy(got_pan, lp_slot(k, r), place_sem.at[1]).wait()
    stores[-2].wait()
    stores[-1].wait()


def exchange(tab, mask, sib_cot, sib_panel, par_cot, par_panel, sib_inverse, par_inverse):
    bf, f32 = jnp.bfloat16, jnp.float32
    srows, scols = sib_inverse.shape
    prows, pcols = par_inverse.shape
    anyspace = pl.BlockSpec(memory_space=pl.ANY)
    vmem = pl.BlockSpec(memory_space=pltpu.VMEM)
    dma = pltpu.SemaphoreType.DMA
    lifted = jax.ShapeDtypeStruct((2, G, G, CAP, PIECE, H), bf)
    return pl.pallas_call(
        exchange_kernel,
        out_shape=(
            jax.ShapeDtypeStruct((prows, pcols), f32),
            lifted,
            lifted,
            jax.ShapeDtypeStruct((H // 2, scols), f32),
            jax.ShapeDtypeStruct((H // 4, pcols), f32),
        ),
        in_specs=[pl.BlockSpec(memory_space=pltpu.SMEM)] + [anyspace] * 7,
        out_specs=(anyspace, anyspace, anyspace, vmem, vmem),
        scratch_shapes=[
            pltpu.VMEM(mask.shape, jnp.int32),
            pltpu.VMEM((SIB, 2 * H), bf),
            pltpu.VMEM((SIB, 2 * H), bf),
            pltpu.VMEM((PAR, 2 * H), bf),
            pltpu.VMEM((srows, scols), bf),
            pltpu.VMEM((prows, pcols), bf),
            pltpu.VMEM((2 * G, SIB, 2 * H), bf),
            pltpu.VMEM((2 * G, PAR, 2 * H), bf),
            pltpu.VMEM((2, G, G, 2, PIECE, H), bf),
            pltpu.VMEM((2 * BLK, BLK), bf),
            pltpu.VMEM((2, 2 * SIB, H), bf),
            pltpu.VMEM((2 * SIB, H), bf),
            pltpu.VMEM((2, PAR, H), bf),
            pltpu.VMEM((PAR, H), bf),
            pltpu.VMEM((2, 3, BLK, H), bf),
            pltpu.VMEM((2, BLK, H), bf),
            pltpu.VMEM((2, 3 * G, PIECE, H), bf),
            pltpu.VMEM((G, 2, PIECE, H), bf),
            pltpu.VMEM((G, CAP, PIECE, H), bf),
            pltpu.VMEM((G, CAP, PIECE, H), bf),
            pltpu.VMEM((G, CAP, PIECE, H), bf),
            pltpu.VMEM((G, CAP, PIECE, H), bf),
            pltpu.VMEM((G, 2, PIECE, H), bf),
            pltpu.VMEM((8, H // 4, pcols), f32),
            pltpu.VMEM((4, H // 2, scols), f32),
            pltpu.VMEM((2, H // 4, pcols), f32),
            pltpu.VMEM((2, H // 4, pcols), f32),
            pltpu.VMEM((2, H // 4, pcols), f32),
            pltpu.VMEM((H // 4, pcols), f32),
            pltpu.VMEM((H // 4, pcols), f32),
            pltpu.VMEM((2, H // 2, scols), f32),
            pltpu.VMEM((H // 2, scols), f32),
            pltpu.VMEM((H // 2, scols), f32),
            pltpu.VMEM((pcols, 2 * H), bf),
            pltpu.VMEM((2, STEP * BLK, pcols), f32),
            dma((5, 8)),
            dma((5, 8)),
            dma((5, 8)),
            dma((5, 8)),
            dma((7,)),
            dma((2,)),
            dma((2,)),
            dma((4,)),
            *[dma((8,))] * 10,
            dma((7,)),
            dma((7,)),
            dma((6,)),
            dma((6,)),
        ],
        compiler_params=pltpu.CompilerParams(
            collective_id=0, has_side_effects=True, vmem_limit_bytes=54 << 20
        ),
    )(tab, mask, sib_cot, sib_panel, par_cot, par_panel, sib_inverse, par_inverse)


def border_kernel(tab, part, *refs):
    lifted, panels, (out, left, right) = refs[: 2 * STEP], refs[2 * STEP : 2 * STEP + 16], refs[2 * STEP + 16 :]
    i = pl.program_id(0)

    def lanes(s, h):
        return slice((2 * s + h) * H, (2 * s + h + 1) * H)

    @pl.when(i == 0)
    def _():
        for b in range(8):
            rows = slice(b * BLK, (b + 1) * BLK)
            for h in range(2):
                for s in range(2):
                    block = panels[s * 8 + b][h, 0, :, 0].reshape(BLK, H)
                    there = tab[COL_TAB + s * 8 + b] >= 0
                    right[rows, lanes(s, h)] = jnp.where(there, block, jnp.zeros_like(block))

    for b in range(STEP):
        rows = slice(b * BLK, (b + 1) * BLK)
        for s in range(2):
            there = tab[ROW_TAB + s * 16 + i * STEP + b] >= 0
            for h in range(2):
                block = lifted[s * STEP + b][h, :, 0].reshape(BLK, H)
                left[rows, lanes(s, h)] = jnp.where(there, block, jnp.zeros_like(block))
    out[...] = -(part[...] + lax.dot_general(left[...], right[...], NT, preferred_element_type=jnp.float32))


def border(tab, part, lc, lp):
    rows, cols = part.shape
    lc = lc.reshape(2, G, G * CAP, PIECE, H)

    def lifted_spec(s, b):
        return pl.BlockSpec(
            (2, G, 1, PIECE, H),
            lambda i, t: (0, 0, jnp.maximum(t[ROW_TAB + s * 16 + i * STEP + b], 0), 0, 0),
        )

    def panel_spec(n):
        def at(i, t):
            slot = jnp.maximum(t[COL_TAB + n], 0)
            return 0, slot // CAP, 0, slot % CAP, 0, 0

        return pl.BlockSpec((2, 1, G, 1, PIECE, H), at, pipeline_mode=pl.Buffered(1))

    return pl.pallas_call(
        border_kernel,
        out_shape=jax.ShapeDtypeStruct((rows, cols), jnp.float32),
        grid_spec=pltpu.PrefetchScalarGridSpec(
            num_scalar_prefetch=1,
            grid=(2 * G // STEP,),
            in_specs=[pl.BlockSpec((STEP * BLK, cols), lambda i, t: (i, 0))]
            + [lifted_spec(s, b) for s in range(2) for b in range(STEP)]
            + [panel_spec(n) for n in range(16)],
            out_specs=pl.BlockSpec((STEP * BLK, cols), lambda i, t: (i, 0)),
            scratch_shapes=[
                pltpu.VMEM((STEP * BLK, 4 * H), jnp.bfloat16),
                pltpu.VMEM((cols, 4 * H), jnp.bfloat16),
            ],
        ),
        compiler_params=pltpu.CompilerParams(vmem_limit_bytes=50 << 20),
    )(tab, part, *([lc] * (2 * STEP)), *([lp] * 16))


def tables(block_map, r, c):
    blocks = 3 * G
    tile_blocks = 2 * G
    ids = block_map.reshape(G, blocks)
    dest = ids // tile_blocks
    iota = jnp.arange(blocks, dtype=jnp.int32)
    tile = jnp.arange(G, dtype=jnp.int32)[:, None]
    before = (dest[:, :, None] == dest[:, None, :]) & (iota[None, None, :] < iota[None, :, None])
    rank = jnp.sum(before.astype(jnp.int32), axis=-1)
    n = jnp.arange(END, dtype=jnp.int32)[:, None, None]
    slot = dest * CAP + rank
    in_slot = (n < ROW_TAB) & (tile == r)[None] & (slot[None] == n)
    s, row_at, col_at = tile // (G // 2), n - ROW_TAB, n - COL_TAB
    in_rows = (n >= ROW_TAB) & (n < COL_TAB) & (s[None] == row_at // 16) & (ids[None] == r * 16 + row_at % 16)
    in_cols = (n >= COL_TAB) & (n < END) & (s[None] == col_at // 8) & (ids[None] == c * 8 + col_at % 8)
    value = jnp.where(in_slot, iota[None, None], 0) + jnp.where(in_rows | in_cols, (tile * CAP + rank + 1)[None], 0)
    flat = n[:, 0, 0]
    return jnp.sum(value, axis=(1, 2)) + jnp.where(flat < ROW_TAB, 0, -1)


def on_device(sib_inverse, sib_panel, sib_cot, par_inverse, par_panel, par_cot, block_map, row_mask):
    r = lax.axis_index("row")
    c = lax.axis_index("col")
    tab = tables(block_map, r, c)
    mask = row_mask.reshape(-1, BLK)
    part, lc, lp, sib_sum, par_sum = exchange(
        tab, mask, sib_cot, sib_panel, par_cot, par_panel, sib_inverse, par_inverse
    )
    return sib_sum.T, par_sum.T, border(tab, part, lc, lp)


def solution(mesh):
    placed = (
        P("row", "col"),
        P(("row", "col"), None),
        P(("row", "col"), None),
        P("row", "col"),
        P(("row", "col"), None),
        P(("row", "col"), None),
        P(),
        P(),
    )
    return jax.shard_map(
        on_device,
        mesh=mesh,
        in_specs=placed,
        out_specs=(P("col", "row"), P("col", "row"), P("row", "col")),
        check_vma=False,
    )
```

time: 118 us -> 105 us (0.89)
  Pallas kernels: 107 us -> 99.3 us
  other arithmetic: 7.47 us -> 1.27 us
    pallas_call x2, Pallas kernels: 107 us -> 99.3 us  [the longest x1 87.5 us: exchange(): pl.pallas_call(exchange_kernel, out_shape=(jax.ShapeDtypeStruct((prows, p...]
    unnamed x1 -> x6, local copies, waits for them, and re-layouts: 0.91 us -> 2.62 us
    neg x3 -> x0, other arithmetic: 1.69 us -> none  [the longest x1 0.93 us: on_device(): -par_panel]
    reduce_sum x4 -> x2, other arithmetic: 2.1 us -> 0.46 us  [the longest x1 0.29 us: tables(): rank = jnp.sum(before.astype(jnp.int32), axis=-1)]
    convert_element_type x2 -> x0, other arithmetic: 1.55 us -> none  [the longest x1 0.78 us: on_device(): lax.dynamic_slice_in_dim(row_mask, (r * 16 + c) * SIB, SIB)]
where the time goes in v2:
time: 105 us
  Pallas kernels  99.3 us (95%)
  local copies, waits for them, and re-layouts  3.38 us (3%)
  other arithmetic  1.27 us (1%)
    pallas_call x1, Pallas kernels, exchange(): pl.pallas_call(exchange_kernel, out_shape=(jax.ShapeDtypeStruct((prows, p...  87.5 us
    pallas_call x1, Pallas kernels, border(): pl.pallas_call(border_kernel, out_shape=jax.ShapeDtypeStruct((rows, cols)...  11.8 us
    unnamed x6, local copies, waits for them, and re-layouts  2.62 us

profile of v2, /device:TPU:1, one launch (start us, length us, event | category | flops | bytes accessed | tf_op | source)
XLA Modules:
  0.0 104.7 jit_solution(15323577088299259846)
XLA Ops:
  0.7 0.1 broadcast_and_fusion
  0.8 0.1 compare_and_fusion.1
  0.9 0.8 reshape.457
  1.6 0.3 convert_reduce_fusion
  1.9 0.1 multiply_add_fusion
  2.0 0.2 add_reduce_fusion
  2.2 0.5 select_add_fusion.tab
  2.7 0.0 copy-start
  2.7 87.5 %shard_map.103 = (f32[2048,1024]{1,0:T(8,128)}, bf16[2,8,8,4,16,256]{5,4,3,2,1,0:T(8,128)(2,1)}, bf16[2,8,8,4,16,256]{5,4,3,2,1,0:T(8,128)(2,1)}, f32[128,768]{1,0:T(8,128)}, f32[64,1024]{1,0:T(8,128)}) custom-call(s32[80]{0:T(128)} %select_add_fusion.tab, s32[192,128]{1,0:T(8,128)} %bitcast.14, bf16[192,512]{1,0:T(8,128)(2,1)} %sib_cot_hbm.1, ...), custom_call_target="tpu_custom_call" | custom-call | tf_op jit(solution)/shard_map/pallas_call | solution.py:517
  90.2 1.9 %copy.12 = f32[768,128]{1,0:T(8,128)} copy(f32[768,128]{0,1:T(8,128)} %bitcast.12) | data formatting | bytes 786432
  92.1 0.0 copy-done
  92.1 0.0 copy-start.1
  92.1 11.8 %shard_map.104 = f32[2048,1024]{1,0:T(8,128)} custom-call(s32[80]{0:T(128)S(1)} %copy-done, f32[2048,1024]{1,0:T(8,128)} %get-tuple-element.10.part, bf16[2,8,32,16,256]{4,3,2,1,0:T(8,128)(2,1)} %bitcast.4, bf16[2,8,32,16,256]{4,3,2,1,0:T(8,128)(2,1)} %bitcast.5, bf16[2,8,32,16,256]{4,3,2,1,0:T(8,128)(2,1)} %bitcast.6, bf16[2,8,32,16,256]{4,3,2,1,0:T(8,128)(2,1)} %bitcast.7, ...), custom_call_target="tpu_custom_call" | custom-call | tf_op jit(solution)/shard_map/pallas_call | solution.py:628
  104.0 0.0 copy-done.1
  104.0 0.7 copy.14
  (9 shorter events, 0.1 us)
Async XLA Ops:
  2.7 89.4 %copy-start = (s32[80]{0:T(128)S(1)}, s32[80]{0:T(128)}, u32[]{:S(2)}) copy-start(s32[80]{0:T(128)} %select_add_fusion.tab) | copy-start | bytes 964
  92.1 11.8 %copy-start.1 = (f32[64,1024]{1,0:T(8,128)S(1)}, f32[64,1024]{1,0:T(8,128)}, u32[]{:S(2)}) copy-start(f32[64,1024]{1,0:T(8,128)} %get-tuple-element.9) | copy-start | bytes 786436

commit v3 on v2

--- a/solution.py
+++ b/solution.py
@@ -429,6 +429,11 @@
         )
         ct[:, :, parts[i]] = part.reshape(4, H // 2, -1)
 
+    r_take(near_l.at[1], 2)
+    r_take(near_r.at[1], 5)
+    zs[...] = pt[piece(0, 1)] + near_l[1] + near_r[1]
+    r_give(zs, zr, 6, mate)
+
     sib_part(0)
     q_give(ct.at[by_xz, :, parts[0]], s_in.at[1, :, parts[0]], 0, mate)
     q_give(ct.at[by_z, :, parts[0]], s_in.at[0, :, parts[0]], 1, mate)
@@ -438,11 +443,12 @@
 
     ag_lp.ring()
     ag_pp.rest()
-
-    r_take(near_l.at[1], 2)
-    r_take(near_r.at[1], 5)
-    zs[...] = pt[piece(0, 1)] + near_l[1] + near_r[1]
-    r_give(zs, zr, 6, mate)
+    q_take(s_in.at[1, :, parts[1]], 2)
+    s_mid[:, parts[1]] = ct[by_z, :, parts[1]] + s_in[1, :, parts[1]]
+    q_give(s_mid.at[:, parts[1]], s_last.at[:, parts[1]], 5, mate)
+    q_take(s_in.at[1, :, parts[0]], 0)
+    s_mid[:, parts[0]] = ct[by_x, :, parts[0]] + s_in[1, :, parts[0]]
+    q_give(s_mid.at[:, parts[0]], s_last.at[:, parts[0]], 4, beside)
 
     ag_pp.halves()
     for n in range(8):
@@ -467,13 +473,7 @@
         stores[t].start()
 
     tile(0)
-    q_take(s_in.at[1, :, parts[1]], 2)
-    s_mid[:, parts[1]] = ct[by_z, :, parts[1]] + s_in[1, :, parts[1]]
-    q_give(s_mid.at[:, parts[1]], s_last.at[:, parts[1]], 5, mate)
     tile(1)
-    q_take(s_in.at[1, :, parts[0]], 0)
-    s_mid[:, parts[0]] = ct[by_x, :, parts[0]] + s_in[1, :, parts[0]]
-    q_give(s_mid.at[:, parts[0]], s_last.at[:, parts[0]], 4, beside)
     tile(2)
     ag_lc.rest()
     ag_lp.rest()
@@ -491,7 +491,7 @@
     for j in range(cols_s // BLK):
         lanes = slice(j * BLK, (j + 1) * BLK)
         keep = mask[pl.ds(first_line + j, 1), :].astype(jnp.float32)
-        sib_out[:, lanes] = -(ct[own, :, lanes] + s_in[0, :, lanes] + s_last[:, lanes]) * keep
+        sib_out[lanes, :] = (-(ct[own, :, lanes] + s_in[0, :, lanes] + s_last[:, lanes]) * keep).T
 
     ag_lc.halves()
     ag_lp.halves()
@@ -520,7 +520,7 @@
             jax.ShapeDtypeStruct((prows, pcols), f32),
             lifted,
             lifted,
-            jax.ShapeDtypeStruct((H // 2, scols), f32),
+            jax.ShapeDtypeStruct((scols, H // 2), f32),
             jax.ShapeDtypeStruct((H // 4, pcols), f32),
         ),
         in_specs=[pl.BlockSpec(memory_space=pltpu.SMEM)] + [anyspace] * 7,
@@ -672,7 +672,7 @@
     part, lc, lp, sib_sum, par_sum = exchange(
         tab, mask, sib_cot, sib_panel, par_cot, par_panel, sib_inverse, par_inverse
     )
-    return sib_sum.T, par_sum.T, border(tab, part, lc, lp)
+    return sib_sum, par_sum.T, border(tab, part, lc, lp)
 
 
 def solution(mesh):

time: 105 us -> 104 us (level)
  local copies, waits for them, and re-layouts: 3.38 us -> 2.22 us
    unnamed x6 -> x8, local copies, waits for them, and re-layouts: 2.62 us -> 1.46 us
where the time goes in v3:
time: 104 us
  Pallas kernels  99.6 us (96%)
  local copies, waits for them, and re-layouts  2.22 us (2%)
  other arithmetic  1.27 us (1%)
    pallas_call x1, Pallas kernels, exchange(): pl.pallas_call(exchange_kernel, out_shape=(jax.ShapeDtypeStruct((prows, p...  87.7 us
    pallas_call x1, Pallas kernels, border(): pl.pallas_call(border_kernel, out_shape=jax.ShapeDtypeStruct((rows, cols)...  11.9 us

profile of v3, /device:TPU:1, one launch (start us, length us, event | category | flops | bytes accessed | tf_op | source)
XLA Modules:
  0.0 103.8 jit_solution(7717887388384748390)
XLA Ops:
  0.7 0.1 broadcast_and_fusion
  0.8 0.1 compare_and_fusion.1
  0.9 0.8 reshape.457
  1.6 0.3 convert_reduce_fusion
  1.9 0.1 multiply_add_fusion
  2.0 0.2 add_reduce_fusion
  2.2 0.5 select_add_fusion.tab
  2.7 0.0 copy-start
  2.7 87.7 %shard_map.103 = (f32[2048,1024]{1,0:T(8,128)}, bf16[2,8,8,4,16,256]{5,4,3,2,1,0:T(8,128)(2,1)}, bf16[2,8,8,4,16,256]{5,4,3,2,1,0:T(8,128)(2,1)}, f32[768,128]{1,0:T(8,128)}, f32[64,1024]{1,0:T(8,128)}) custom-call(s32[80]{0:T(128)} %select_add_fusion.tab, s32[192,128]{1,0:T(8,128)} %bitcast.12, bf16[192,512]{1,0:T(8,128)(2,1)} %sib_cot_hbm.1, ...), custom_call_target="tpu_custom_call" | custom-call | tf_op jit(solution)/shard_map/pallas_call | solution.py:517
  90.3 0.0 copy-done
  90.4 0.0 copy-start.1
  90.4 0.0 copy-start.2
  90.4 11.9 %shard_map.104 = f32[2048,1024]{1,0:T(8,128)} custom-call(s32[80]{0:T(128)S(1)} %copy-done, f32[2048,1024]{1,0:T(8,128)} %get-tuple-element.10.part, bf16[2,8,32,16,256]{4,3,2,1,0:T(8,128)(2,1)} %bitcast.3, bf16[2,8,32,16,256]{4,3,2,1,0:T(8,128)(2,1)} %bitcast.4, bf16[2,8,32,16,256]{4,3,2,1,0:T(8,128)(2,1)} %bitcast.5, bf16[2,8,32,16,256]{4,3,2,1,0:T(8,128)(2,1)} %bitcast.6, ...), custom_call_target="tpu_custom_call" | custom-call | tf_op jit(solution)/shard_map/pallas_call | solution.py:628
  102.3 0.0 copy-done.1
  102.3 0.7 copy.13
  103.1 0.0 copy-done.2
  103.1 0.7 copy.14
  (9 shorter events, 0.1 us)
Async XLA Ops:
  2.7 87.7 %copy-start = (s32[80]{0:T(128)S(1)}, s32[80]{0:T(128)}, u32[]{:S(2)}) copy-start(s32[80]{0:T(128)} %select_add_fusion.tab) | copy-start | bytes 964
  90.4 11.9 %copy-start.1 = (f32[768,128]{1,0:T(8,128)S(1)}, f32[768,128]{1,0:T(8,128)}, u32[]{:S(2)}) copy-start(f32[768,128]{1,0:T(8,128)} %get-tuple-element.26) | copy-start | bytes 1179652
  90.4 12.7 %copy-start.2 = (f32[64,1024]{1,0:T(8,128)S(1)}, f32[64,1024]{1,0:T(8,128)}, u32[]{:S(2)}) copy-start(f32[64,1024]{1,0:T(8,128)} %get-tuple-element.9) | copy-start | bytes 786436
